TPU v7x, 32 devices: a whole 2x2x4 slice. The times are simulated.
32 devices in a mesh: groups: 2 (over y), ctx: 4 (over z), heads: 4 (over x, core).
Axes of the slice: x: 2, y: 2, z: 4, core: 2. Of those that a mesh axis runs over, the one named last changes fastest.
Arguments:
- queries: bfloat16 [2048, 4096], P(('groups', 'ctx'), 'heads'), parts along dimension 0
- keys: bfloat16 [2048, 1024], P(('groups', 'ctx'), 'heads'), parts along dimension 0
- values: bfloat16 [2048, 1024], P(('groups', 'ctx'), 'heads'), parts along dimension 0, may hold values from -6 to 6
- conv_kernel: float32 [32, 6, 11], P('heads')
- head_mix: float32 [8, 4, 4], P('heads')
- norm_gain: float32 [4096], P('heads'), may hold values from 0.5 to 1.5
- bounds: int32 [4], P('groups'), parts along dimension 0, may hold values from 0 to 1024, as said below
Outputs:
- attended: bfloat16 [2048, 4096], P(('groups', 'ctx'), 'heads'), parts along dimension 0
There are 2 independent parts, one for each index of `groups`. A program takes and returns all parts, laid end to end along the dimension named above; an argument that names none is the same for every part. Nothing has to cross between parts.
Inputs may be any that keep to these rules, and one draw needn't show every extreme that they name: bounds[0] < bounds[1], and bounds[1] >= 512.
All inputs are finite; a program needn't handle non-finite values.
Results may differ from a plain program's by a relative error of at most 0.0045.
Values may be sent and summed in bfloat16 or wider, within the bound.
No kernel may reach another device: no remote copies, remote signals or barrier semaphores. Data moves between devices by JAX's collectives and lax.ppermute only.
A program may use at most 64 MiB of HBM per device.

v0:
```python
import jax
import jax.numpy as jnp
from jax import lax
from jax.sharding import PartitionSpec as P

NEG_FILL = -1e30
EPSILON = 1e-06


def from_behind(value, axis, steps):
    count = lax.axis_size(axis)
    leading, last = (max(0, -steps), min(count, count - steps))
    return lax.ppermute(value, axis, [(source, source + steps) for source in range(leading, last)])


def conv_scores(zeroed, kernel, out_rows, out_cols, q_edge, k_edge):
    summed = jnp.zeros(zeroed.shape[:2] + (out_rows, out_cols), jnp.float32)
    for tap_row in range(kernel.shape[2]):
        for tap_col in range(kernel.shape[3]):
            summed = (
                summed
                + kernel[:, :, tap_row, tap_col][:, :, None, None]
                * zeroed[
                    :,
                    :,
                    q_edge - tap_row : q_edge - tap_row + out_rows,
                    2 * k_edge - tap_col : 2 * k_edge - tap_col + out_cols,
                ]
            )
    return summed


def per_device(queries, keys, values, conv_kernel, head_mix, norm_gain, bounds):
    num_rows = queries.shape[0]
    kv_local = head_mix.shape[0]
    heads_per_group = head_mix.shape[1]
    head_width = keys.shape[1] // kv_local
    q_taps = conv_kernel.shape[1]
    k_taps = conv_kernel.shape[2]
    q_edge = q_taps - 1
    k_edge = k_taps // 2
    score_scale = head_width ** (-0.5)
    ctx_size = lax.axis_size("ctx")
    row_first = lax.axis_index("ctx") * num_rows
    start_row = bounds[0]
    end_row = bounds[1]
    prior_rows = from_behind(queries[num_rows - q_edge :], "ctx", 1)
    query_ext = jnp.concatenate([prior_rows, queries], 0).reshape(
        num_rows + q_edge, kv_local, heads_per_group, head_width
    )
    kernel = conv_kernel.reshape(kv_local, heads_per_group, q_taps, k_taps)
    seg_rows = query_ext.shape[0] - q_edge
    ext_pos = row_first - q_edge + jnp.arange(seg_rows + q_edge, dtype=jnp.int32)
    pos = row_first + jnp.arange(seg_rows, dtype=jnp.int32)
    live = (pos >= start_row) & (pos < end_row)
    segments = ((query_ext, ext_pos, pos, live),)

    def attend(carry_state, segment, key_block, value_block, key_first):
        seg_queries, row_ext_pos, row_pos, row_live = segment
        seg_rows = row_pos.shape[0]
        run_max, run_sum, run_acc = carry_state
        key_count = value_block.shape[0]
        raw_scores = (
            jnp.einsum("rgmd,kgd->gmrk", seg_queries, key_block, preferred_element_type=jnp.float32)
            * score_scale
        )
        key_ext_pos = key_first - k_edge + jnp.arange(key_count + 2 * k_edge, dtype=jnp.int32)
        zeroed = jnp.where(key_ext_pos[None, :] <= row_ext_pos[:, None], raw_scores, 0.0)
        mixed_scores = conv_scores(zeroed, kernel, seg_rows, key_count, q_edge, k_edge)
        key_pos = key_first + jnp.arange(key_count, dtype=jnp.int32)
        valid_mask = (key_pos[None, :] <= row_pos[:, None]) & row_live[:, None]
        block_max = jnp.max(jnp.where(valid_mask, mixed_scores, NEG_FILL), axis=-1)
        new_max = jnp.maximum(run_max, block_max)
        weights = jnp.where(valid_mask, jnp.exp(mixed_scores - new_max[..., None]), 0.0)
        factor = jnp.exp(run_max - new_max)
        new_sum = run_sum * factor + jnp.sum(weights, axis=-1)
        product = jnp.einsum(
            "gmrk,kgd->rgmd",
            weights.astype(jnp.bfloat16),
            value_block,
            preferred_element_type=jnp.float32,
        )
        new_acc = run_acc * jnp.transpose(factor, (2, 0, 1))[..., None] + product
        return (new_max, new_sum, new_acc)

    def guarded(carry_state, segment, key_block, value_block, key_first):
        return attend(carry_state, segment, key_block, value_block, key_first)

    def guarded_all(states, key_block, value_block, key_first):
        return tuple(
            (
                guarded(states[idx], segments[idx], key_block, value_block, key_first)
                for idx in range(len(segments))
            )
        )

    def fresh_state(segment):
        seg_rows = segment[2].shape[0]
        return (
            jnp.full((kv_local, heads_per_group, seg_rows), NEG_FILL, jnp.float32),
            jnp.zeros((kv_local, heads_per_group, seg_rows), jnp.float32),
            jnp.zeros((seg_rows, kv_local, heads_per_group, head_width), jnp.float32),
        )

    initial = tuple((fresh_state(segment) for segment in segments))
    boundary = jnp.concatenate([keys[:k_edge], keys[num_rows - k_edge :]], 0)
    edge_table = lax.all_gather(boundary, "ctx", axis=0, tiled=True)
    edge_table = edge_table.reshape(ctx_size, 2 * k_edge, kv_local * head_width)
    blank_rows = jnp.zeros((1, 2 * k_edge, kv_local * head_width), keys.dtype)
    padded_table = jnp.concatenate([blank_rows, edge_table, blank_rows], 0)
    key_piece = lax.all_gather(keys, "ctx", axis=0, tiled=True)
    value_piece = lax.all_gather(values, "ctx", axis=0, tiled=True)
    shards = key_piece.shape[0] // num_rows
    key_split = key_piece.reshape(shards, num_rows, kv_local, head_width)
    value_split = value_piece.reshape(shards, num_rows, kv_local, head_width)

    def per_shard(shard_pos, inner_state):
        lower_edge = lax.dynamic_index_in_dim(padded_table, shard_pos, 0, keepdims=False)[k_edge:]
        upper_edge = lax.dynamic_index_in_dim(padded_table, shard_pos + 2, 0, keepdims=False)[
            :k_edge
        ]
        middle_keys = lax.dynamic_index_in_dim(key_split, shard_pos, 0, keepdims=False)
        block_keys = jnp.concatenate(
            [
                lower_edge.reshape(k_edge, kv_local, head_width),
                middle_keys,
                upper_edge.reshape(k_edge, kv_local, head_width),
            ],
            0,
        )
        block_values = lax.dynamic_index_in_dim(value_split, shard_pos, 0, keepdims=False)
        return guarded_all(inner_state, block_keys, block_values, shard_pos * num_rows)

    final_states = lax.fori_loop(0, shards, per_shard, initial)
    run_max, run_sum, run_acc = final_states[0]
    row_live = segments[0][3]
    seg_rows = row_live.shape[0]
    divisor = jnp.where(row_live[None, None, :], run_sum, 1.0)
    probs_out = run_acc / jnp.transpose(divisor, (2, 0, 1))[..., None]
    blended = jnp.einsum("gab,rgbd->rgad", head_mix, probs_out, precision=lax.Precision.HIGHEST)
    mean_sq = jnp.mean(blended * blended, axis=-1, keepdims=True)
    normed = (
        blended
        * lax.rsqrt(mean_sq + EPSILON)
        * norm_gain.reshape(kv_local, heads_per_group, head_width)
    )
    result = jnp.where(row_live[:, None, None, None], normed, 0.0)
    return result.reshape(seg_rows, kv_local * heads_per_group * head_width).astype(jnp.bfloat16)


def solution(mesh):
    return jax.shard_map(
        per_device,
        mesh=mesh,
        in_specs=(
            P(("groups", "ctx"), "heads"),
            P(("groups", "ctx"), "heads"),
            P(("groups", "ctx"), "heads"),
            P("heads", None, None),
            P("heads", None, None),
            P("heads"),
            P("groups"),
        ),
        out_specs=P(("groups", "ctx"), "heads"),
        check_vma=False,
    )
```

profile of v0, /device:TPU:0, one launch (start us, length us, event | category | flops | bytes accessed | tf_op | source)
XLA Modules:
  0.0 266.3 jit_solution(12256957341839974469)
XLA Ops:
  0.0 0.8 slice.1361
  0.8 4.9 %collective-permute-start = (bf16[5,1024]{1,0:T(8,128)(2,1)S(1)}, bf16[5,1024]{1,0:T(8,128)(2,1)S(1)}, u32[]{:S(2)}, u32[]{:S(2)}) collective-permute-start(bf16[5,1024]{1,0:T(8,128)(2,1)S(1)} %slice.1361), channel_id=1, source_target_pairs={{0,4},{4,8},{8,12},{1,5},{5,9},{9,13},{2,6},{6,10},{10,14},{3,7},{... | collective-permute-start | bytes 30728 | tf_op jit(solution)/shard_map/ppermute | solution.py:13
  5.8 0.7 fusion.89
  6.5 16.0 %all_gather.10 = bf16[1024,256]{1,0:T(8,128)(2,1)S(1)} all-gather(bf16[256,256]{1,0:T(8,128)(2,1)} %param.10), channel_id=1, replica_groups=mesh['groups'=2,'ctx'=4,'heads'=4] {'ctx'}, dimensions={0}, use_global_device_ids=true | all-gather | bytes 655360 | tf_op jit(solution)/shard_map/all_gather | solution.py:111
  22.4 13.1 %all-gather = bf16[4,10,256]{2,1,0:T(8,128)(2,1)S(1)} all-gather(bf16[1,10,256]{2,1,0:T(8,128)(2,1)S(1)} %maximum_bitcast_fusion.2), channel_id=1, replica_groups=mesh['groups'=2,'ctx'=4,'heads'=4] {'ctx'}, dimensions={0}, use_global_device_ids=true | all-gather | bytes 25600 | tf_op jit(solution)/shard_map/all_gather | solution.py:107
  35.6 1.3 fusion.90
  36.9 14.9 %all_gather.11 = bf16[1024,256]{1,0:T(8,128)(2,1)S(1)} all-gather(bf16[256,256]{1,0:T(8,128)(2,1)} %param.11), channel_id=1, replica_groups=mesh['groups'=2,'ctx'=4,'heads'=4] {'ctx'}, dimensions={0}, use_global_device_ids=true | all-gather | bytes 655360 | tf_op jit(solution)/shard_map/all_gather | solution.py:112
  51.8 1.7 compare_and_fusion.2
  53.6 0.9 reshape.80
  54.5 0.9 reshape.82
  55.7 0.3 reshape.81
  56.0 0.9 copy.34
  56.9 201.9 %while.22 = (s32[]{:T(128)}, f32[2,4,256]{2,1,0:T(4,128)S(1)}, f32[2,4,256]{2,1,0:T(4,128)S(1)}, f32[256,2,4,128]{0,3,2,1:T(8,128)}, f32[2,4,6,11]{1,0,3,2:T(2,1...) while((s32[]{:T(128)}, f32[2,4,256]{2,1,0:T(4,128)S(1)}, ...), condition=%wide.region_3.4_spmd.clone.clone.clone, body=%wide.region_0.3_spmd.clone.clone.clone.sunk | while | flops 351798912 | bytes 160064880 | solution.py:134
  56.9 1.2 constant_dynamic-slice_fusion.3
  58.0 0.7 copy.51
  58.9 1.9 bitcast_select_fusion.2
  60.7 1.2 compare_and_fusion.5
  62.1 0.7 slice_bitcast_fusion.70
  62.8 0.7 slice_bitcast_fusion.71
  63.4 0.7 slice_bitcast_fusion.72
  64.1 0.6 slice_bitcast_fusion.73
  64.7 38.1 %select_reduce_fusion.2 = (f32[2,4,256]{2,1,0:T(4,128)S(1)}, f32[2,4,256,256]{3,2,1,0:T(8,128)}) fusion(pred[256,256]{1,0:T(8,128)(4,1)S(1)} %compare_and_fusion.6, f32[2,4,261,266]{3,2,1,0:T(8,128)S(1)} %bitcast_select_fusion.2, f32[2,4]{1,0:T(2,128)S(1)} %get-tuple-element.735, f32[2,4]{1,0:T(2,128)S(1)} %get-tuple-element.736, ...), kind=kLoop, calls=%fused_computation.136.clone.1 | loop fusion | flops 69728256 | bytes 140585024 | tf_op jit(solution)/shard_map/while/body/eval_jaxpr/reduce_max | solution.py:72
  103.0 3.3 %fusion.106 = f32[256,2,4,128]{0,3,2,1:T(8,128)} fusion(f32[2,4,256,256]{3,2,1,0:T(8,128)} %get-tuple-element.803, f32[256,2,4,128]{0,3,2,1:T(8,128)} %get-tuple-element.829, f32[2,4,256]{2,1,0:T(4,128)S(1)} %get-tuple-element.847, pred[256,256]{1,0:T(8,128)(4,1)S(1)} %compare_and_fusion.6, f32[256,2,4]{0,2,1:T(4,128)S(1)} %get-tuple-element.804, ...), kind=kOutput, calls=%fused_computation.140.clone.1 | convolution fusion | flops 136577024 | bytes 4407297 | tf_op jit(solution)/shard_map/while/body/eval_jaxpr/gmrk,kgd->rgmd/dot_general | solution.py:77
  106.3 0.7 fusion.104
  107.2 1.2 constant_dynamic-slice_fusion.3
  108.3 0.7 copy.51
  109.2 1.9 bitcast_select_fusion.2
  111.0 1.2 compare_and_fusion.5
  112.4 0.7 slice_bitcast_fusion.70
  113.1 0.7 slice_bitcast_fusion.71
  113.7 0.7 slice_bitcast_fusion.72
  114.4 0.6 slice_bitcast_fusion.73
  115.0 38.1 %select_reduce_fusion.2 = (f32[2,4,256]{2,1,0:T(4,128)S(1)}, f32[2,4,256,256]{3,2,1,0:T(8,128)}) fusion(pred[256,256]{1,0:T(8,128)(4,1)S(1)} %compare_and_fusion.6, f32[2,4,261,266]{3,2,1,0:T(8,128)S(1)} %bitcast_select_fusion.2, f32[2,4]{1,0:T(2,128)S(1)} %get-tuple-element.735, f32[2,4]{1,0:T(2,128)S(1)} %get-tuple-element.736, ...), kind=kLoop, calls=%fused_computation.136.clone.1 | loop fusion | flops 69728256 | bytes 140585024 | tf_op jit(solution)/shard_map/while/body/eval_jaxpr/reduce_max | solution.py:72
  153.3 3.6 %fusion.106 = f32[256,2,4,128]{0,3,2,1:T(8,128)} fusion(f32[2,4,256,256]{3,2,1,0:T(8,128)} %get-tuple-element.803, f32[256,2,4,128]{0,3,2,1:T(8,128)} %get-tuple-element.829, f32[2,4,256]{2,1,0:T(4,128)S(1)} %get-tuple-element.847, pred[256,256]{1,0:T(8,128)(4,1)S(1)} %compare_and_fusion.6, f32[256,2,4]{0,2,1:T(4,128)S(1)} %get-tuple-element.804, ...), kind=kOutput, calls=%fused_computation.140.clone.1 | convolution fusion | flops 136577024 | bytes 4407297 | tf_op jit(solution)/shard_map/while/body/eval_jaxpr/gmrk,kgd->rgmd/dot_general | solution.py:77
  156.9 0.7 fusion.104
  157.7 1.2 constant_dynamic-slice_fusion.3
  158.9 0.7 copy.51
  159.7 1.9 bitcast_select_fusion.2
  161.6 1.2 compare_and_fusion.5
  163.0 0.7 slice_bitcast_fusion.70
  163.6 0.7 slice_bitcast_fusion.71
  164.3 0.7 slice_bitcast_fusion.72
  165.0 0.6 slice_bitcast_fusion.73
  165.6 38.1 %select_reduce_fusion.2 = (f32[2,4,256]{2,1,0:T(4,128)S(1)}, f32[2,4,256,256]{3,2,1,0:T(8,128)}) fusion(pred[256,256]{1,0:T(8,128)(4,1)S(1)} %compare_and_fusion.6, f32[2,4,261,266]{3,2,1,0:T(8,128)S(1)} %bitcast_select_fusion.2, f32[2,4]{1,0:T(2,128)S(1)} %get-tuple-element.735, f32[2,4]{1,0:T(2,128)S(1)} %get-tuple-element.736, ...), kind=kLoop, calls=%fused_computation.136.clone.1 | loop fusion | flops 69728256 | bytes 140585024 | tf_op jit(solution)/shard_map/while/body/eval_jaxpr/reduce_max | solution.py:72
  203.8 3.6 %fusion.106 = f32[256,2,4,128]{0,3,2,1:T(8,128)} fusion(f32[2,4,256,256]{3,2,1,0:T(8,128)} %get-tuple-element.803, f32[256,2,4,128]{0,3,2,1:T(8,128)} %get-tuple-element.829, f32[2,4,256]{2,1,0:T(4,128)S(1)} %get-tuple-element.847, pred[256,256]{1,0:T(8,128)(4,1)S(1)} %compare_and_fusion.6, f32[256,2,4]{0,2,1:T(4,128)S(1)} %get-tuple-element.804, ...), kind=kOutput, calls=%fused_computation.140.clone.1 | convolution fusion | flops 136577024 | bytes 4407297 | tf_op jit(solution)/shard_map/while/body/eval_jaxpr/gmrk,kgd->rgmd/dot_general | solution.py:77
  207.4 0.7 fusion.104
  208.3 1.2 constant_dynamic-slice_fusion.3
  209.5 0.7 copy.51
  210.3 1.9 bitcast_select_fusion.2
  212.1 1.2 compare_and_fusion.5
  213.5 0.7 slice_bitcast_fusion.70
  214.2 0.7 slice_bitcast_fusion.71
  214.9 0.7 slice_bitcast_fusion.72
  215.5 0.6 slice_bitcast_fusion.73
  216.1 38.1 %select_reduce_fusion.2 = (f32[2,4,256]{2,1,0:T(4,128)S(1)}, f32[2,4,256,256]{3,2,1,0:T(8,128)}) fusion(pred[256,256]{1,0:T(8,128)(4,1)S(1)} %compare_and_fusion.6, f32[2,4,261,266]{3,2,1,0:T(8,128)S(1)} %bitcast_select_fusion.2, f32[2,4]{1,0:T(2,128)S(1)} %get-tuple-element.735, f32[2,4]{1,0:T(2,128)S(1)} %get-tuple-element.736, ...), kind=kLoop, calls=%fused_computation.136.clone.1 | loop fusion | flops 69728256 | bytes 140585024 | tf_op jit(solution)/shard_map/while/body/eval_jaxpr/reduce_max | solution.py:72
  254.4 3.6 %fusion.106 = f32[256,2,4,128]{0,3,2,1:T(8,128)} fusion(f32[2,4,256,256]{3,2,1,0:T(8,128)} %get-tuple-element.803, f32[256,2,4,128]{0,3,2,1:T(8,128)} %get-tuple-element.829, f32[2,4,256]{2,1,0:T(4,128)S(1)} %get-tuple-element.847, pred[256,256]{1,0:T(8,128)(4,1)S(1)} %compare_and_fusion.6, f32[256,2,4]{0,2,1:T(4,128)S(1)} %get-tuple-element.804, ...), kind=kOutput, calls=%fused_computation.140.clone.1 | convolution fusion | flops 136577024 | bytes 4407297 | tf_op jit(solution)/shard_map/while/body/eval_jaxpr/gmrk,kgd->rgmd/dot_general | solution.py:77
  258.0 0.7 fusion.104
  258.8 0.6 select_bitcast_fusion
  259.4 1.3 broadcast_divide_fusion
  260.7 0.4 copy.36
  261.1 2.3 multiply_reduce_fusion
  263.5 1.5 select_convert_fusion
  265.0 0.3 copy.39
  265.3 1.0 copy.40
  (84 shorter events, 2.2 us)
Async XLA Ops:
  0.0 261.1 %copy-start = (f32[2,4,4]{2,1,0:T(4,128)S(1)}, f32[2,4,4]{2,1,0:T(4,128)}, u32[]{:S(2)}) copy-start(f32[2,4,4]{2,1,0:T(4,128)} %param.13) | copy-start | bytes 388
  0.0 55.5 %copy-start.2 = (bf16[256,1024]{1,0:T(8,128)(2,1)S(1)}, bf16[256,1024]{1,0:T(8,128)(2,1)}, u32[]{:S(2)}) copy-start(bf16[256,1024]{1,0:T(8,128)(2,1)} %param.9) | copy-start | bytes 1572868
  0.0 55.4 %copy-start.5 = (f32[8,6,11]{2,0,1:T(8,128)S(1)}, f32[8,6,11]{2,0,1:T(8,128)}, u32[]{:S(2)}) copy-start(f32[8,6,11]{2,0,1:T(8,128)} %param.12) | copy-start | bytes 6340
  0.8 54.7 %collective-permute-start = (bf16[5,1024]{1,0:T(8,128)(2,1)S(1)}, bf16[5,1024]{1,0:T(8,128)(2,1)S(1)}, u32[]{:S(2)}, u32[]{:S(2)}) collective-permute-start(bf16[5,1024]{1,0:T(8,128)(2,1)S(1)} %slice.1361), channel_id=1, source_target_pairs={{0,4},{4,8},{8,12},{1,5},{5,9},{9,13},{2,6},{6,10},{10,14},{3,7},{... | collective-permute-start | bytes 30728 | tf_op jit(solution)/shard_map/ppermute | solution.py:13
  56.9 2.0 copy-start.3
  103.0 3.4 %copy-start.1 = (f32[2,4,256,256]{3,2,1,0:T(8,128)S(1)}, f32[2,4,256,256]{3,2,1,0:T(8,128)}, u32[]{:S(2)}) copy-start(f32[2,4,256,256]{3,2,1,0:T(8,128)} %get-tuple-element.803) | copy-start | bytes 6291460 | tf_op jit(solution)/shard_map/while
  106.3 0.8 copy-start.4
  107.1 2.0 copy-start.3
  153.3 3.6 %copy-start.1 = (f32[2,4,256,256]{3,2,1,0:T(8,128)S(1)}, f32[2,4,256,256]{3,2,1,0:T(8,128)}, u32[]{:S(2)}) copy-start(f32[2,4,256,256]{3,2,1,0:T(8,128)} %get-tuple-element.803) | copy-start | bytes 6291460 | tf_op jit(solution)/shard_map/while
  156.9 0.8 copy-start.4
  157.7 2.0 copy-start.3
  203.8 3.6 %copy-start.1 = (f32[2,4,256,256]{3,2,1,0:T(8,128)S(1)}, f32[2,4,256,256]{3,2,1,0:T(8,128)}, u32[]{:S(2)}) copy-start(f32[2,4,256,256]{3,2,1,0:T(8,128)} %get-tuple-element.803) | copy-start | bytes 6291460 | tf_op jit(solution)/shard_map/while
  207.4 0.8 copy-start.4
  208.2 2.0 copy-start.3
  254.4 3.6 %copy-start.1 = (f32[2,4,256,256]{3,2,1,0:T(8,128)S(1)}, f32[2,4,256,256]{3,2,1,0:T(8,128)}, u32[]{:S(2)}) copy-start(f32[2,4,256,256]{3,2,1,0:T(8,128)} %get-tuple-element.803) | copy-start | bytes 6291460 | tf_op jit(solution)/shard_map/while
  258.0 0.8 copy-start.4
  260.7 2.8 %copy-start.6 = (pred[256]{0:T(512)(128)(4,1)S(1)}, pred[256]{0:T(512)(128)(4,1)}, u32[]{:S(2)}) copy-start(pred[256]{0:T(512)(128)(4,1)} %compare_and_fusion.2) | copy-start | bytes 772
  260.7 2.8 %copy-start.7 = (f32[1024]{0:T(1024)S(1)}, f32[1024]{0:T(1024)}, u32[]{:S(2)}) copy-start(f32[1024]{0:T(1024)} %param.14) | copy-start | bytes 12292
where the time goes:
time: 267 us; the launch traced here: 266 us
  other arithmetic  167 us (63%)
  blocking collectives  44 us (16%)
  local copies, waits for them, and re-layouts  26 us (10%)
  matrix products  23.9 us (9%)
  starting transfers between devices  4.95 us (2%)
    reduce_max x4, other arithmetic, attend(): block_max = jnp.max(jnp.where(valid_mask, mixed_scores, NEG_FILL), axis=-1)  152 us
    all_gather x1, blocking collectives, per_device(): key_piece = lax.all_gather(keys, 'ctx', axis=0, tiled=True)  16 us
    all_gather x1, blocking collectives, per_device(): value_piece = lax.all_gather(values, 'ctx', axis=0, tiled=True)  14.9 us
    dot_general x4, matrix products, attend(): jnp.einsum('gmrk,kgd->rgmd', weights.astype(jnp.bfloat16), value_block, p...  14.2 us
    all_gather x1, blocking collectives, per_device(): edge_table = lax.all_gather(boundary, 'ctx', axis=0, tiled=True)  13.1 us
    mul x16, local copies, waits for them, and re-layouts, conv_scores(): kernel[:, :, tap_row, tap_col][:, :, None, None]  10.4 us
    dot_general x4, matrix products, attend(): jnp.einsum('rgmd,kgd->gmrk', seg_queries, key_block, preferred_element_ty...  7.42 us
    and x5, other arithmetic, per_device(): live = (pos >= start_row) & (pos < end_row)  6.71 us
  transfers between devices with their start and end apart: 1, of which 0 were waited for; matrix products, arithmetic and copies ran while one was open for 2% of the time, Pallas kernels for 0%

commit v1 on v0

--- a/solution.py
+++ b/solution.py
@@ -1,3 +1,4 @@
+import functools
 import jax
 import jax.numpy as jnp
 from jax import lax
@@ -5,6 +6,34 @@
 
 NEG_FILL = -1e30
 EPSILON = 1e-06
+
+
+def start_seats_all_for(t0, which_dim):
+    res = list(t0.shape[1:])
+    res[which_dim] *= t0.shape[0]
+    prior = jnp.moveaxis(t0, 0, which_dim).reshape(res)
+    return prior
+
+
+def prepare_object(inputs, lane_axis):
+    tmp, answer = (lax.axis_size(lane_axis), lax.axis_index(lane_axis))
+    local_part, plain = (inputs[None], 1)
+    while plain < tmp:
+        upper = lax.ppermute(local_part, lane_axis, [(dd, dd ^ plain) for dd in range(tmp)])
+        met_up = answer & plain == 0
+        local_part = jnp.concatenate(
+            [jnp.where(met_up, local_part, upper), jnp.where(met_up, upper, local_part)]
+        )
+        plain *= 2
+    return local_part
+
+
+def fix_view(work_x, vec, array_dim):
+    latest = start_seats_all_for(prepare_object(work_x, vec), array_dim)
+    return latest
+
+
+lead_the_edges = functools.partial(fix_view, vec="ctx", array_dim=0)
 
 
 def from_behind(value, axis, steps):
@@ -108,7 +137,7 @@
     edge_table = edge_table.reshape(ctx_size, 2 * k_edge, kv_local * head_width)
     blank_rows = jnp.zeros((1, 2 * k_edge, kv_local * head_width), keys.dtype)
     padded_table = jnp.concatenate([blank_rows, edge_table, blank_rows], 0)
-    key_piece = lax.all_gather(keys, "ctx", axis=0, tiled=True)
+    key_piece = lead_the_edges(keys)
     value_piece = lax.all_gather(values, "ctx", axis=0, tiled=True)
     shards = key_piece.shape[0] // num_rows
     key_split = key_piece.reshape(shards, num_rows, kv_local, head_width)

time: 267 us -> 246 us (0.921)
  blocking collectives: 44 us -> 29.3 us
  other arithmetic: 167 us -> 159 us
  local copies, waits for them, and re-layouts: 26 us -> 22.7 us
  waiting for transfers between devices: 0.01 us -> 2.87 us
    all_gather x1 -> x0, blocking collectives: 16 us -> none  [per_device(): key_piece = lax.all_gather(keys, 'ctx', axis=0, tiled=True)]
    reduce_max x4, other arithmetic: 152 us -> 144 us  [attend(): block_max = jnp.max(jnp.where(valid_mask, mixed_scores, NEG_FILL), axis=-1)]
    mul x16, local copies, waits for them, and re-layouts: 10.4 us -> 4.95 us  [conv_scores(): kernel[:, :, tap_row, tap_col][:, :, None, None]]
    ppermute x0 -> x2, starting transfers between devices: none -> 5.07 us  [prepare_object(): lax.ppermute(local_part, lane_axis, [(dd, dd ^ plain) for dd in range(tmp)])]
    ppermute x1, starting transfers between devices: 4.95 us -> 1.91 us  [from_behind(): lax.ppermute(value, axis, [(source, source + steps) for source in range(l...]
    ppermute x0 -> x2, waiting for transfers between devices: none -> 2.87 us  [prepare_object(): lax.ppermute(local_part, lane_axis, [(dd, dd ^ plain) for dd in range(tmp)])]
  transfers between devices with their start and end apart: 1 -> 3, of which waited for: 0 -> 1; matrix products, arithmetic and copies ran while one was open for 2% -> 3% of each run, Pallas kernels for 0% -> 0%
where the time goes in v1:
time: 246 us
  other arithmetic  159 us (65%)
  blocking collectives  29.3 us (12%)
  matrix products  23.7 us (10%)
  local copies, waits for them, and re-layouts  22.7 us (9%)
  starting transfers between devices  6.98 us (3%)
  waiting for transfers between devices  2.87 us (1%)
    reduce_max x4, other arithmetic, attend(): block_max = jnp.max(jnp.where(valid_mask, mixed_scores, NEG_FILL), axis=-1)  144 us
    all_gather x1, blocking collectives, per_device(): value_piece = lax.all_gather(values, 'ctx', axis=0, tiled=True)  16.1 us
    dot_general x4, matrix products, attend(): jnp.einsum('gmrk,kgd->rgmd', weights.astype(jnp.bfloat16), value_block, p...  14.2 us
    all_gather x1, blocking collectives, per_device(): edge_table = lax.all_gather(boundary, 'ctx', axis=0, tiled=True)  13.2 us
    dot_general x4, matrix products, attend(): jnp.einsum('rgmd,kgd->gmrk', seg_queries, key_block, preferred_element_ty...  7.26 us
    and x5, other arithmetic, per_device(): live = (pos >= start_row) & (pos < end_row)  6.82 us
    ppermute x2, starting transfers between devices, prepare_object(): lax.ppermute(local_part, lane_axis, [(dd, dd ^ plain) for dd in range(tmp)])  5.07 us
    mul x16, local copies, waits for them, and re-layouts, conv_scores(): kernel[:, :, tap_row, tap_col][:, :, None, None]  4.95 us
  transfers between devices with their start and end apart: 3, of which 1 were waited for; matrix products, arithmetic and copies ran while one was open for 3% of the time, Pallas kernels for 0%

profile of v1, /device:TPU:0, one launch (start us, length us, event | category | flops | bytes accessed | tf_op | source)
XLA Modules:
  0.0 245.8 jit_solution(1284739310500842121)
XLA Ops:
  0.0 1.1 copy.35
  1.1 3.1 %collective-permute-start = (bf16[1,256,256]{1,2,0:T(8,128)(2,1)S(1)}, bf16[1,256,256]{1,2,0:T(8,128)(2,1)S(1)}, u32[]{:S(2)}, u32[]{:S(2)}) collective-permute-start(bf16[1,256,256]{1,2,0:T(8,128)(2,1)S(1)} %bitcast.207), channel_id=1, source_target_pairs={{0,4},{4,0},{8,12},{12,8},{1,5},{5,1},{9,13},{13,9},{2,6},{6,2},{1... | collective-permute-start | bytes 393224 | tf_op jit(solution)/shard_map/ppermute | solution.py:22
  4.2 0.7 slice.1361
  4.9 1.9 collective-permute-start.2
  6.8 0.7 fusion.89
  7.6 16.1 %all_gather.7 = bf16[1024,256]{1,0:T(8,128)(2,1)S(1)} all-gather(bf16[256,256]{1,0:T(8,128)(2,1)} %param.11), channel_id=1, replica_groups=mesh['groups'=2,'ctx'=4,'heads'=4] {'ctx'}, dimensions={0}, use_global_device_ids=true | all-gather | bytes 655360 | tf_op jit(solution)/shard_map/all_gather | solution.py:141
  23.7 13.2 %all-gather = bf16[4,10,256]{2,1,0:T(8,128)(2,1)S(1)} all-gather(bf16[1,10,256]{2,1,0:T(8,128)(2,1)S(1)} %maximum_bitcast_fusion.2), channel_id=1, replica_groups=mesh['groups'=2,'ctx'=4,'heads'=4] {'ctx'}, dimensions={0}, use_global_device_ids=true | all-gather | bytes 25600 | tf_op jit(solution)/shard_map/all_gather | solution.py:136
  37.0 1.9 collective-permute-start.1
  38.9 0.6 fusion.90
  39.6 1.7 compare_and_fusion.2
  41.3 0.9 reshape.78
  42.2 0.8 copy.36
  43.1 0.3 reshape.77
  43.4 0.9 copy.38
  44.3 2.9 %collective-permute-done.1 = bf16[2,256,256]{1,2,0:T(8,128)(2,1)S(1)} collective-permute-done((bf16[2,256,256]{1,2,0:T(8,128)(2,1)S(1)}, bf16[2,256,256]{1,2,0:T(8,128)(2,1)S(1)}, u32[]{:S(2)}, u32[]{:S(2)}) %collective-permute-start.1) | collective-permute-done | bytes 262176 | tf_op jit(solution)/shard_map/ppermute | solution.py:22
  47.2 190.9 %while.22 = (s32[]{:T(128)}, f32[2,4,256]{2,1,0:T(4,128)S(1)}, f32[2,4,256]{2,1,0:T(4,128)}, f32[256,2,4,128]{0,3,2,1:T(8,128)}, f32[2,4,6,11]{1,0,3,2:T(2,128)}...) while((s32[]{:T(128)}, f32[2,4,256]{2,1,0:T(4,128)S(1)}, ...), condition=%wide.region_3.4_spmd.clone.clone.clone, body=%wide.region_0.3_spmd.clone.clone.clone.sunk | while | flops 351798912 | bytes 164333328 | solution.py:163
  47.3 0.7 dynamic-slice_bitcast_fusion.3
  48.3 1.8 bitcast_select_fusion.2
  50.1 1.3 compare_and_fusion.5
  51.4 0.1 compare_and_fusion.6
  51.6 0.6 slice_bitcast_fusion.72
  52.2 0.6 slice_bitcast_fusion.73
  52.8 36.1 %select_reduce_fusion.2 = (f32[2,4,256]{2,1,0:T(4,128)S(1)}, f32[2,4,256,256]{3,2,1,0:T(8,128)}) fusion(pred[256,256]{1,0:T(8,128)(4,1)S(1)} %compare_and_fusion.6, f32[2,4,261,266]{3,2,1,0:T(8,128)S(1)} %bitcast_select_fusion.2, f32[2,4]{1,0:T(2,128)S(1)} %get-tuple-element.734, f32[2,4]{1,0:T(2,128)S(1)} %get-tuple-element.735, ...), kind=kLoop, calls=%fused_computation.136.clone.1 | loop fusion | flops 69728256 | bytes 140585024 | tf_op jit(solution)/shard_map/while/body/eval_jaxpr/reduce_max | solution.py:101
  88.9 1.0 constant_dynamic-slice_fusion.5
  90.1 3.3 %fusion.106 = f32[256,2,4,128]{0,3,2,1:T(8,128)} fusion(f32[2,4,256,256]{3,2,1,0:T(8,128)} %get-tuple-element.802, f32[256,2,4,128]{0,3,2,1:T(8,128)} %get-tuple-element.827, f32[2,4,256]{2,1,0:T(4,128)S(1)} %get-tuple-element.845, pred[256,256]{1,0:T(8,128)(4,1)S(1)} %compare_and_fusion.6, f32[256,2,4]{0,2,1:T(4,128)S(1)} %get-tuple-element.803, ...), kind=kOutput, calls=%fused_computation.140.clone.1 | convolution fusion | flops 136577024 | bytes 4407297 | tf_op jit(solution)/shard_map/while/body/eval_jaxpr/gmrk,kgd->rgmd/dot_general | solution.py:106
  93.4 0.7 fusion.104
  94.2 0.6 copy-done.7
  94.8 0.7 dynamic-slice_bitcast_fusion.3
  95.8 1.8 bitcast_select_fusion.2
  97.7 1.3 compare_and_fusion.5
  99.1 0.6 slice_bitcast_fusion.72
  99.7 0.6 slice_bitcast_fusion.73
  100.3 36.1 %select_reduce_fusion.2 = (f32[2,4,256]{2,1,0:T(4,128)S(1)}, f32[2,4,256,256]{3,2,1,0:T(8,128)}) fusion(pred[256,256]{1,0:T(8,128)(4,1)S(1)} %compare_and_fusion.6, f32[2,4,261,266]{3,2,1,0:T(8,128)S(1)} %bitcast_select_fusion.2, f32[2,4]{1,0:T(2,128)S(1)} %get-tuple-element.734, f32[2,4]{1,0:T(2,128)S(1)} %get-tuple-element.735, ...), kind=kLoop, calls=%fused_computation.136.clone.1 | loop fusion | flops 69728256 | bytes 140585024 | tf_op jit(solution)/shard_map/while/body/eval_jaxpr/reduce_max | solution.py:101
  136.4 1.0 constant_dynamic-slice_fusion.5
  137.6 3.6 %fusion.106 = f32[256,2,4,128]{0,3,2,1:T(8,128)} fusion(f32[2,4,256,256]{3,2,1,0:T(8,128)} %get-tuple-element.802, f32[256,2,4,128]{0,3,2,1:T(8,128)} %get-tuple-element.827, f32[2,4,256]{2,1,0:T(4,128)S(1)} %get-tuple-element.845, pred[256,256]{1,0:T(8,128)(4,1)S(1)} %compare_and_fusion.6, f32[256,2,4]{0,2,1:T(4,128)S(1)} %get-tuple-element.803, ...), kind=kOutput, calls=%fused_computation.140.clone.1 | convolution fusion | flops 136577024 | bytes 4407297 | tf_op jit(solution)/shard_map/while/body/eval_jaxpr/gmrk,kgd->rgmd/dot_general | solution.py:106
  141.2 0.7 fusion.104
  142.0 0.6 copy-done.7
  142.6 0.7 dynamic-slice_bitcast_fusion.3
  143.6 1.8 bitcast_select_fusion.2
  145.4 1.3 compare_and_fusion.5
  146.9 0.6 slice_bitcast_fusion.72
  147.5 0.6 slice_bitcast_fusion.73
  148.1 36.1 %select_reduce_fusion.2 = (f32[2,4,256]{2,1,0:T(4,128)S(1)}, f32[2,4,256,256]{3,2,1,0:T(8,128)}) fusion(pred[256,256]{1,0:T(8,128)(4,1)S(1)} %compare_and_fusion.6, f32[2,4,261,266]{3,2,1,0:T(8,128)S(1)} %bitcast_select_fusion.2, f32[2,4]{1,0:T(2,128)S(1)} %get-tuple-element.734, f32[2,4]{1,0:T(2,128)S(1)} %get-tuple-element.735, ...), kind=kLoop, calls=%fused_computation.136.clone.1 | loop fusion | flops 69728256 | bytes 140585024 | tf_op jit(solution)/shard_map/while/body/eval_jaxpr/reduce_max | solution.py:101
  184.2 1.0 constant_dynamic-slice_fusion.5
  185.4 3.6 %fusion.106 = f32[256,2,4,128]{0,3,2,1:T(8,128)} fusion(f32[2,4,256,256]{3,2,1,0:T(8,128)} %get-tuple-element.802, f32[256,2,4,128]{0,3,2,1:T(8,128)} %get-tuple-element.827, f32[2,4,256]{2,1,0:T(4,128)S(1)} %get-tuple-element.845, pred[256,256]{1,0:T(8,128)(4,1)S(1)} %compare_and_fusion.6, f32[256,2,4]{0,2,1:T(4,128)S(1)} %get-tuple-element.803, ...), kind=kOutput, calls=%fused_computation.140.clone.1 | convolution fusion | flops 136577024 | bytes 4407297 | tf_op jit(solution)/shard_map/while/body/eval_jaxpr/gmrk,kgd->rgmd/dot_general | solution.py:106
  189.0 0.7 fusion.104
  189.8 0.6 copy-done.7
  190.4 0.7 dynamic-slice_bitcast_fusion.3
  191.4 1.8 bitcast_select_fusion.2
  193.2 1.3 compare_and_fusion.5
  194.7 0.6 slice_bitcast_fusion.72
  195.3 0.6 slice_bitcast_fusion.73
  195.9 36.1 %select_reduce_fusion.2 = (f32[2,4,256]{2,1,0:T(4,128)S(1)}, f32[2,4,256,256]{3,2,1,0:T(8,128)}) fusion(pred[256,256]{1,0:T(8,128)(4,1)S(1)} %compare_and_fusion.6, f32[2,4,261,266]{3,2,1,0:T(8,128)S(1)} %bitcast_select_fusion.2, f32[2,4]{1,0:T(2,128)S(1)} %get-tuple-element.734, f32[2,4]{1,0:T(2,128)S(1)} %get-tuple-element.735, ...), kind=kLoop, calls=%fused_computation.136.clone.1 | loop fusion | flops 69728256 | bytes 140585024 | tf_op jit(solution)/shard_map/while/body/eval_jaxpr/reduce_max | solution.py:101
  232.0 1.0 constant_dynamic-slice_fusion.5
  233.1 3.6 %fusion.106 = f32[256,2,4,128]{0,3,2,1:T(8,128)} fusion(f32[2,4,256,256]{3,2,1,0:T(8,128)} %get-tuple-element.802, f32[256,2,4,128]{0,3,2,1:T(8,128)} %get-tuple-element.827, f32[2,4,256]{2,1,0:T(4,128)S(1)} %get-tuple-element.845, pred[256,256]{1,0:T(8,128)(4,1)S(1)} %compare_and_fusion.6, f32[256,2,4]{0,2,1:T(4,128)S(1)} %get-tuple-element.803, ...), kind=kOutput, calls=%fused_computation.140.clone.1 | convolution fusion | flops 136577024 | bytes 4407297 | tf_op jit(solution)/shard_map/while/body/eval_jaxpr/gmrk,kgd->rgmd/dot_general | solution.py:106
  236.7 0.7 fusion.104
  237.5 0.6 copy-done.7
  238.1 0.7 select_bitcast_fusion
  238.8 1.3 broadcast_divide_fusion
  240.2 0.4 copy.40
  240.6 2.3 multiply_reduce_fusion
  243.0 1.5 select_convert_fusion
  244.5 0.3 copy.43
  244.8 1.0 copy.44
  (137 shorter events, 2.7 us)
Async XLA Ops:
  0.0 240.6 %copy-start = (f32[2,4,4]{2,1,0:T(4,128)S(1)}, f32[2,4,4]{2,1,0:T(4,128)}, u32[]{:S(2)}) copy-start(f32[2,4,4]{2,1,0:T(4,128)} %param.13) | copy-start | bytes 388
  0.0 43.0 %copy-start.5 = (bf16[256,1024]{1,0:T(8,128)(2,1)S(1)}, bf16[256,1024]{1,0:T(8,128)(2,1)}, u32[]{:S(2)}) copy-start(bf16[256,1024]{1,0:T(8,128)(2,1)} %param.9) | copy-start | bytes 1572868
  0.0 38.9 %copy-start.13 = (s32[2]{0:T(128)S(1)}, s32[2]{0:T(128)}, u32[]{:S(2)}) copy-start(s32[2]{0:T(128)} %param.15) | copy-start | bytes 28
  0.0 42.2 %copy-start.10 = (f32[8,6,11]{2,0,1:T(8,128)S(1)}, f32[8,6,11]{2,0,1:T(8,128)}, u32[]{:S(2)}) copy-start(f32[8,6,11]{2,0,1:T(8,128)} %param.12) | copy-start | bytes 6340
  1.1 35.8 %collective-permute-start = (bf16[1,256,256]{1,2,0:T(8,128)(2,1)S(1)}, bf16[1,256,256]{1,2,0:T(8,128)(2,1)S(1)}, u32[]{:S(2)}, u32[]{:S(2)}) collective-permute-start(bf16[1,256,256]{1,2,0:T(8,128)(2,1)S(1)} %bitcast.207), channel_id=1, source_target_pairs={{0,4},{4,0},{8,12},{12,8},{1,5},{5,1},{9,13},{13,9},{2,6},{6,2},{1... | collective-permute-start | bytes 393224 | tf_op jit(solution)/shard_map/ppermute | solution.py:22
  4.9 38.1 %collective-permute-start.2 = (bf16[5,1024]{1,0:T(8,128)(2,1)S(1)}, bf16[5,1024]{1,0:T(8,128)(2,1)S(1)}, u32[]{:S(2)}, u32[]{:S(2)}) collective-permute-start(bf16[5,1024]{1,0:T(8,128)(2,1)S(1)} %slice.1361), channel_id=1, source_target_pairs={{0,4},{4,8},{8,12},{1,5},{5,9},{9,13},{2,6},{6,10},{10,14},{3,7},{... | collective-permute-start | bytes 30728 | tf_op jit(solution)/shard_map/ppermute | solution.py:42
  37.0 10.1 %collective-permute-start.1 = (bf16[2,256,256]{1,2,0:T(8,128)(2,1)S(1)}, bf16[2,256,256]{1,2,0:T(8,128)(2,1)S(1)}, u32[]{:S(2)}, u32[]{:S(2)}) collective-permute-start(bf16[2,256,256]{1,2,0:T(8,128)(2,1)S(1)} %pad_maximum_fusion.2), channel_id=1, source_target_pairs={{0,8},{4,12},{8,0},{12,4},{1,9},{5,13},{9,1},{13,5},{2,10},{6,14},... | collective-permute-start | bytes 786440 | tf_op jit(solution)/shard_map/ppermute | solution.py:22
  47.3 1.0 copy-start.2
  47.3 1.0 copy-start.8
  48.3 3.3 %copy-start.4 = (f32[2,4,6,11]{1,0,3,2:T(2,128)S(1)}, f32[2,4,6,11]{1,0,3,2:T(2,128)}, u32[]{:S(2)}) copy-start(f32[2,4,6,11]{1,0,3,2:T(2,128)} %get-tuple-element.848) | copy-start | bytes 6340 | tf_op jit(solution)/shard_map/while
  90.1 3.4 %copy-start.1 = (f32[2,4,256,256]{3,2,1,0:T(8,128)S(1)}, f32[2,4,256,256]{3,2,1,0:T(8,128)}, u32[]{:S(2)}) copy-start(f32[2,4,256,256]{3,2,1,0:T(8,128)} %get-tuple-element.802) | copy-start | bytes 6291460 | tf_op jit(solution)/shard_map/while
  93.4 0.8 copy-start.6
  93.4 1.4 copy-start.3
  93.4 1.4 copy-start.9
  94.2 0.6 copy-start.7
  94.8 1.0 copy-start.2
  94.8 1.0 copy-start.8
  95.8 3.3 %copy-start.4 = (f32[2,4,6,11]{1,0,3,2:T(2,128)S(1)}, f32[2,4,6,11]{1,0,3,2:T(2,128)}, u32[]{:S(2)}) copy-start(f32[2,4,6,11]{1,0,3,2:T(2,128)} %get-tuple-element.848) | copy-start | bytes 6340 | tf_op jit(solution)/shard_map/while
  137.6 3.6 %copy-start.1 = (f32[2,4,256,256]{3,2,1,0:T(8,128)S(1)}, f32[2,4,256,256]{3,2,1,0:T(8,128)}, u32[]{:S(2)}) copy-start(f32[2,4,256,256]{3,2,1,0:T(8,128)} %get-tuple-element.802) | copy-start | bytes 6291460 | tf_op jit(solution)/shard_map/while
  141.2 0.8 copy-start.6
  141.2 1.4 copy-start.3
  141.2 1.4 copy-start.9
  142.0 0.6 copy-start.7
  142.6 1.0 copy-start.2
  142.6 1.0 copy-start.8
  143.6 3.3 %copy-start.4 = (f32[2,4,6,11]{1,0,3,2:T(2,128)S(1)}, f32[2,4,6,11]{1,0,3,2:T(2,128)}, u32[]{:S(2)}) copy-start(f32[2,4,6,11]{1,0,3,2:T(2,128)} %get-tuple-element.848) | copy-start | bytes 6340 | tf_op jit(solution)/shard_map/while
  185.3 3.6 %copy-start.1 = (f32[2,4,256,256]{3,2,1,0:T(8,128)S(1)}, f32[2,4,256,256]{3,2,1,0:T(8,128)}, u32[]{:S(2)}) copy-start(f32[2,4,256,256]{3,2,1,0:T(8,128)} %get-tuple-element.802) | copy-start | bytes 6291460 | tf_op jit(solution)/shard_map/while
  189.0 0.8 copy-start.6
  189.0 1.4 copy-start.3
  189.0 1.4 copy-start.9
  189.7 0.6 copy-start.7
  190.4 1.0 copy-start.2
  190.4 1.0 copy-start.8
  191.3 3.3 %copy-start.4 = (f32[2,4,6,11]{1,0,3,2:T(2,128)S(1)}, f32[2,4,6,11]{1,0,3,2:T(2,128)}, u32[]{:S(2)}) copy-start(f32[2,4,6,11]{1,0,3,2:T(2,128)} %get-tuple-element.848) | copy-start | bytes 6340 | tf_op jit(solution)/shard_map/while
  233.1 3.6 %copy-start.1 = (f32[2,4,256,256]{3,2,1,0:T(8,128)S(1)}, f32[2,4,256,256]{3,2,1,0:T(8,128)}, u32[]{:S(2)}) copy-start(f32[2,4,256,256]{3,2,1,0:T(8,128)} %get-tuple-element.802) | copy-start | bytes 6291460 | tf_op jit(solution)/shard_map/while
  236.7 0.8 copy-start.6
  236.7 1.4 copy-start.3
  236.7 1.4 copy-start.9
  237.5 0.6 copy-start.7
  240.2 2.8 %copy-start.11 = (pred[256]{0:T(512)(128)(4,1)S(1)}, pred[256]{0:T(512)(128)(4,1)}, u32[]{:S(2)}) copy-start(pred[256]{0:T(512)(128)(4,1)} %compare_and_fusion.2) | copy-start | bytes 772
  240.2 2.8 %copy-start.12 = (f32[1024]{0:T(1024)S(1)}, f32[1024]{0:T(1024)}, u32[]{:S(2)}) copy-start(f32[1024]{0:T(1024)} %param.14) | copy-start | bytes 12292
